TPU v7x, 32 devices: a whole 2x2x4 slice. The times are simulated.
32 devices in a mesh: lat: 8 (over z, y), lev: 4 (over x, core).
Axes of the slice: x: 2, y: 2, z: 4, core: 2. Of those that a mesh axis runs over, the one named last changes fastest.
Arguments:
- tracer: float32 [2, 4, 384, 1152], P(None, 'lev', 'lat'), may hold values from 0.1 to 2
- east_courant: float32 [4, 384, 1152], P('lev', 'lat'), may hold values from -0.8 to 0.8
- north_courant: float32 [4, 384, 1152], P('lev', 'lat'), may hold values from -0.8 to 0.8
- fall_speed: float32 [2, 4, 384, 1152], P(None, 'lev', 'lat'), may hold values from 0.05 to 0.6
Outputs:
- tracer_out: float32 [2, 4, 384, 1152], P(None, 'lev', 'lat')
- deposit: float32 [2, 384, 1152], P(None, 'lat', 'lev')
All inputs are finite; a program needn't handle non-finite values.
Results may differ from a plain program's by a relative error of at most 0.0003.
Values sent between devices are 32-bit elements; how exact they have to be, the bound alone decides.
No kernel may reach another device: no remote copies, remote signals or barrier semaphores. Data moves between devices by JAX's collectives and lax.ppermute only.
A program may use at most 64 MiB of HBM per device.

v0:
```python
import jax
import jax.numpy as jnp
from jax import lax
from jax.sharding import PartitionSpec as P

HSUB = 4
SETTLE_SUBSTEPS = 6


def passed_along(block, axis, distance):
    devices = range(lax.axis_size(axis))
    route = [(i - distance, i) for i in devices if i - distance in devices]
    return lax.ppermute(block, axis, route)


def extended(block, sides, width):
    for axis, dim in sides:
        count = lax.axis_size(axis)
        forward = [(i, i + 1) for i in range(count - 1)]
        backward = [(target, source) for source, target in forward]
        low = lax.ppermute(
            lax.slice_in_dim(block, block.shape[dim] - width, None, axis=dim), axis, forward
        )
        high = lax.ppermute(lax.slice_in_dim(block, 0, width, axis=dim), axis, backward)
        block = jnp.concatenate([low, block, high], axis=dim)
    return block


def limiter_face_value(outer_west, inner_west, inner_east, outer_east):
    interp = 7.0 / 12.0 * (inner_west + inner_east) - 1.0 / 12.0 * (outer_west + outer_east)
    return jnp.clip(
        interp, jnp.minimum(inner_west, inner_east), jnp.maximum(inner_west, inner_east)
    )


def window_for_cell(source, start, length, axis_dim):
    return lax.slice_in_dim(source, start, start + length, axis=axis_dim)


def sweep(halo_padded_field, courant, axis_dim):
    cells = halo_padded_field.shape[axis_dim] - 6
    faces = limiter_face_value(
        window_for_cell(halo_padded_field, 0, cells + 3, axis_dim),
        window_for_cell(halo_padded_field, 1, cells + 3, axis_dim),
        window_for_cell(halo_padded_field, 2, cells + 3, axis_dim),
        window_for_cell(halo_padded_field, 3, cells + 3, axis_dim),
    )
    middle = window_for_cell(halo_padded_field, 2, cells + 2, axis_dim)
    west_face = window_for_cell(faces, 0, cells + 2, axis_dim)
    east_face = window_for_cell(faces, 1, cells + 2, axis_dim)
    spread = east_face - west_face
    curvature = 6.0 * middle - 3.0 * (west_face + east_face)
    courant_abs = jnp.abs(courant)
    shape_term = 1.0 - 2.0 / 3.0 * courant_abs
    from_west = window_for_cell(east_face, 0, cells + 1, axis_dim) - 0.5 * courant_abs * (
        window_for_cell(spread, 0, cells + 1, axis_dim)
        - shape_term * window_for_cell(curvature, 0, cells + 1, axis_dim)
    )
    from_east = window_for_cell(west_face, 1, cells + 1, axis_dim) + 0.5 * courant_abs * (
        window_for_cell(spread, 1, cells + 1, axis_dim)
        + shape_term * window_for_cell(curvature, 1, cells + 1, axis_dim)
    )
    face_flux_values = courant * jnp.where(courant >= 0, from_west, from_east)
    return window_for_cell(halo_padded_field, 3, cells, axis_dim) - (
        window_for_cell(face_flux_values, 1, cells, axis_dim)
        - window_for_cell(face_flux_values, 0, cells, axis_dim)
    )


def zonal(field, east_courant):
    last_dim = field.ndim - 1
    width = field.shape[last_dim]
    halo_padded_field = jnp.concatenate(
        [
            window_for_cell(field, width - 3, 3, last_dim),
            field,
            window_for_cell(field, 0, 3, last_dim),
        ],
        last_dim,
    )
    cour_dim = east_courant.ndim - 1
    courant = jnp.concatenate(
        [window_for_cell(east_courant, width - 1, 1, cour_dim), east_courant], cour_dim
    )
    return sweep(halo_padded_field, courant, last_dim)


def settle_flat(column_mass, fall_speed):
    deposit = jnp.zeros_like(column_mass[:, 0])
    for settle_substep in range(SETTLE_SUBSTEPS):
        speeds = fall_speed * (1.0 + 0.5 * jnp.tanh(column_mass))
        face_flux_values = speeds * column_mass
        inflow = jnp.concatenate(
            [jnp.zeros_like(face_flux_values[:, :1]), face_flux_values[:, :-1]], 1
        )
        column_mass = column_mass + inflow - face_flux_values
        deposit = deposit + face_flux_values[:, -1]
    return (column_mass, deposit)


def columns_settle(split_portions):
    column_mass, speed_piece = split_portions
    shape_full = column_mass.shape
    flat_shape = (shape_full[0], shape_full[1], shape_full[2] * shape_full[3])
    settled, deposit = settle_flat(column_mass.reshape(flat_shape), speed_piece.reshape(flat_shape))
    returned = lax.all_to_all(
        settled.reshape(shape_full), "lev", split_axis=1, concat_axis=3, tiled=True
    )
    return (returned, deposit.reshape((shape_full[0], shape_full[2], shape_full[3])))


def on_device(tracer, east_courant, north_courant, fall_speed):
    band_rows = tracer.shape[2]
    all_rows = band_rows * lax.axis_size("lat")
    first_row = lax.axis_index("lat") * band_rows
    row_ids = first_row + jnp.arange(band_rows, dtype=jnp.int32)
    north_faces = jnp.where(
        (row_ids == all_rows - 1)[None, :, None], jnp.zeros_like(north_courant), north_courant
    )
    southern_row = passed_along(north_faces[:, band_rows - 1 :, :], "lat", 1)
    face_cour = jnp.concatenate([southern_row, north_faces], 1)
    field = tracer
    for settle_substep in range(HSUB):
        field = zonal(field, east_courant)
        halo_padded_field = extended(field, (("lat", 2),), 3)
        field = sweep(halo_padded_field, face_cour, 2)
    field, deposit = columns_settle(
        (
            lax.all_to_all(field, "lev", split_axis=3, concat_axis=1, tiled=True),
            lax.all_to_all(fall_speed, "lev", split_axis=3, concat_axis=1, tiled=True),
        )
    )
    field = zonal(field, east_courant)
    halo_padded_field = extended(field, (("lat", 2),), 3)
    field = sweep(halo_padded_field, face_cour, 2)
    return (field, deposit)


def solution(mesh):
    in_specs = (
        P(None, "lev", "lat", None),
        P("lev", "lat", None),
        P("lev", "lat", None),
        P(None, "lev", "lat", None),
    )
    out_specs = (P(None, "lev", "lat", None), P(None, "lat", "lev"))
    return jax.shard_map(
        on_device, mesh=mesh, in_specs=in_specs, out_specs=out_specs, check_vma=False
    )
```

profile of v0, /device:TPU:0, one launch (start us, length us, event | category | flops | bytes accessed | tf_op | source)
XLA Modules:
  0.0 129.7 jit_solution(10379016936662951680)
XLA Ops:
  0.7 1.1 broadcast_select_fusion
  1.8 4.9 %collective-permute-start = (f32[1,1,1152]{2,1,0:T(1,128)S(1)}, f32[1,1,1152]{2,1,0:T(1,128)S(1)}, u32[]{:S(2)}, u32[]{:S(2)}) collective-permute-start(f32[1,1,1152]{2,1,0:T(1,128)S(1)} %slice.702), channel_id=1, source_target_pairs={{0,4},{4,8},{8,12},{12,16},{16,20},{20,24},{24,28},{1,5},{5,9},{9,... | collective-permute-start | bytes 13832 | tf_op jit(solution)/shard_map/ppermute | solution.py:13
  6.7 0.8 fusion.153
  7.5 1.1 fusion.141
  8.6 1.1 abs_multiply_fusion.1
  10.2 0.5 fusion.113
  10.6 0.3 slice_subtract_fusion.9
  11.0 0.5 fusion.105
  11.7 3.4 %collective-permute-start.1 = (f32[2,1,3,1152]{3,2,1,0:T(4,128)S(1)}, f32[2,1,3,1152]{3,2,1,0:T(4,128)S(1)}, u32[]{:S(2)}, u32[]{:S(2)}) collective-permute-start(f32[2,1,3,1152]{3,2,1,0:T(4,128)S(1)} %get-tuple-element.46), channel_id=1, source_target_pairs={{0,4},{4,8},{8,12},{12,16},{16,20},{20,24},{24,28},{1,5},{5,9},{9,... | collective-permute-start | bytes 82952 | tf_op jit(solution)/shard_map/ppermute | solution.py:21
  15.1 1.3 collective-permute-start.2
  16.7 4.2 %collective-permute-done.2 = f32[2,1,3,1152]{3,2,1,0:T(4,128)S(1)} collective-permute-done((f32[2,1,3,1152]{3,2,1,0:T(4,128)S(1)}, f32[2,1,3,1152]{3,2,1,0:T(4,128)S(1)}, u32[]{:S(2)}, u32[]{:S(2)}) %collective-permute-start.2) | collective-permute-done | bytes 27680 | tf_op jit(solution)/shard_map/ppermute | solution.py:24
  22.2 0.5 fusion.117
  22.7 0.3 slice_subtract_fusion.8
  23.0 0.5 fusion.96
  23.7 4.3 %collective-permute-start.3 = (f32[2,1,3,1152]{3,2,1,0:T(4,128)S(1)}, f32[2,1,3,1152]{3,2,1,0:T(4,128)S(1)}, u32[]{:S(2)}, u32[]{:S(2)}) collective-permute-start(f32[2,1,3,1152]{3,2,1,0:T(4,128)S(1)} %get-tuple-element.42), channel_id=1, source_target_pairs={{0,4},{4,8},{8,12},{12,16},{16,20},{20,24},{24,28},{1,5},{5,9},{9,... | collective-permute-start | bytes 82952 | tf_op jit(solution)/shard_map/ppermute | solution.py:21
  28.0 1.3 collective-permute-start.4
  29.6 4.2 %collective-permute-done.4 = f32[2,1,3,1152]{3,2,1,0:T(4,128)S(1)} collective-permute-done((f32[2,1,3,1152]{3,2,1,0:T(4,128)S(1)}, f32[2,1,3,1152]{3,2,1,0:T(4,128)S(1)}, u32[]{:S(2)}, u32[]{:S(2)}) %collective-permute-start.4) | collective-permute-done | bytes 27680 | tf_op jit(solution)/shard_map/ppermute | solution.py:24
  35.1 0.5 fusion.121
  35.9 0.5 fusion.87
  36.6 3.4 %collective-permute-start.5 = (f32[2,1,3,1152]{3,2,1,0:T(4,128)S(1)}, f32[2,1,3,1152]{3,2,1,0:T(4,128)S(1)}, u32[]{:S(2)}, u32[]{:S(2)}) collective-permute-start(f32[2,1,3,1152]{3,2,1,0:T(4,128)S(1)} %get-tuple-element.38), channel_id=1, source_target_pairs={{0,4},{4,8},{8,12},{12,16},{16,20},{20,24},{24,28},{1,5},{5,9},{9,... | collective-permute-start | bytes 82952 | tf_op jit(solution)/shard_map/ppermute | solution.py:21
  40.0 1.3 collective-permute-start.6
  41.3 0.4 collective-permute-done.5
  41.8 4.1 %collective-permute-done.6 = f32[2,1,3,1152]{3,2,1,0:T(4,128)S(1)} collective-permute-done((f32[2,1,3,1152]{3,2,1,0:T(4,128)S(1)}, f32[2,1,3,1152]{3,2,1,0:T(4,128)S(1)}, u32[]{:S(2)}, u32[]{:S(2)}) %collective-permute-start.6) | collective-permute-done | bytes 27680 | tf_op jit(solution)/shard_map/ppermute | solution.py:24
  47.1 0.5 fusion.125
  47.9 0.5 fusion.78
  48.6 4.3 %collective-permute-start.7 = (f32[2,1,3,1152]{3,2,1,0:T(4,128)S(1)}, f32[2,1,3,1152]{3,2,1,0:T(4,128)S(1)}, u32[]{:S(2)}, u32[]{:S(2)}) collective-permute-start(f32[2,1,3,1152]{3,2,1,0:T(4,128)S(1)} %get-tuple-element.34), channel_id=1, source_target_pairs={{0,4},{4,8},{8,12},{12,16},{16,20},{20,24},{24,28},{1,5},{5,9},{9,... | collective-permute-start | bytes 82952 | tf_op jit(solution)/shard_map/ppermute | solution.py:21
  52.9 1.5 %collective-permute-start.8 = (f32[2,1,3,1152]{3,2,1,0:T(4,128)S(1)}, f32[2,1,3,1152]{3,2,1,0:T(4,128)S(1)}, u32[]{:S(2)}, u32[]{:S(2)}) collective-permute-start(f32[2,1,3,1152]{3,2,1,0:T(4,128)S(1)} %get-tuple-element.35), channel_id=1, source_target_pairs={{4,0},{8,4},{12,8},{16,12},{20,16},{24,20},{28,24},{5,1},{9,5},{13... | collective-permute-start | bytes 82952 | tf_op jit(solution)/shard_map/ppermute | solution.py:24
  54.4 2.0 %copy.56 = f32[2,1,48,1152]{2,0,1,3:T(2,128)S(1)} copy(f32[2,1,48,1152]{3,2,1,0:T(8,128)} %param.7) | data formatting | bytes 884736 | tf_op args[3]
  56.4 2.9 %reshape.594 = f32[4,1,27648]{2,1,0:T(1,128)} reshape(f32[1152,1,2,48]{3,2,1,0:T(2,128)S(1)} %bitcast.40) | data formatting | bytes 884736
  59.3 4.1 %all-to-all-start.1 = ((f32[4,1,27648]{2,1,0:T(1,128)}), f32[4,1,27648]{2,1,0:T(1,128)}, u32[]{:S(2)}, u32[]{:S(2)}) async-start(f32[4,1,27648]{2,1,0:T(1,128)} %reshape.594), calls=%async_computation.1 | async-start | bytes 884736 | tf_op jit(solution)/shard_map/all_to_all | solution.py:130
  64.3 1.1 copy.54
  65.4 2.8 %reshape.596 = f32[4,1,27648]{2,1,0:T(1,128)} reshape(f32[1152,1,2,48]{3,2,1,0:T(2,128)S(1)} %bitcast.37) | data formatting | bytes 884736
  68.3 3.1 %all-to-all-done.1 = f32[4,1,27648]{2,1,0:T(1,128)} async-done(((f32[4,1,27648]{2,1,0:T(1,128)}), f32[4,1,27648]{2,1,0:T(1,128)}, u32[]{:S(2)}, u32[]{:S(2)}) %all-to-all-start.1) | async-done | bytes 442400 | tf_op jit(solution)/shard_map/all_to_all | solution.py:130
  71.4 4.1 %all-to-all-start = ((f32[4,1,27648]{2,1,0:T(1,128)}), f32[4,1,27648]{2,1,0:T(1,128)}, u32[]{:S(2)}, u32[]{:S(2)}) async-start(f32[4,1,27648]{2,1,0:T(1,128)} %reshape.596), calls=%async_computation | async-start | bytes 884736 | tf_op jit(solution)/shard_map/all_to_all | solution.py:129
  75.5 0.5 broadcast.305
  76.0 2.8 %reduce.2 = f32[4,27648]{1,0:T(4,128)S(1)} reduce(f32[4,1,27648]{2,1,0:T(1,128)} %all-to-all-done.1, f32[]{:T(128)} %broadcast.305), dimensions={1}, to_apply=%all_to_all.38.reduce_sub_computation | reduce | bytes 884740 | tf_op jit(solution)/shard_map/all_to_all | solution.py:130
  78.8 1.9 %reshape.595 = f32[1152,1,2,48]{3,2,1,0:T(2,128)S(1)} reshape(f32[4,27648]{1,0:T(4,128)S(1)} %reduce.2) | data formatting | bytes 884736
  80.8 0.6 copy.57
  81.4 0.5 reshape.590
  81.8 1.7 %all-to-all-done = f32[4,1,27648]{2,1,0:T(1,128)} async-done(((f32[4,1,27648]{2,1,0:T(1,128)}), f32[4,1,27648]{2,1,0:T(1,128)}, u32[]{:S(2)}, u32[]{:S(2)}) %all-to-all-start) | async-done | bytes 442400 | tf_op jit(solution)/shard_map/all_to_all | solution.py:129
  83.5 3.6 %reduce.3 = f32[4,27648]{1,0:T(4,128)} reduce(f32[4,1,27648]{2,1,0:T(1,128)} %all-to-all-done, f32[]{:T(128)} %broadcast.305), dimensions={1}, to_apply=%all_to_all.35.reduce_sub_computation | reduce | bytes 884740 | tf_op jit(solution)/shard_map/all_to_all | solution.py:129
  87.1 2.9 %reshape.597 = f32[1152,1,2,48]{3,2,1,0:T(2,128)S(1)} reshape(f32[4,27648]{1,0:T(4,128)} %reduce.3) | data formatting | bytes 884736
  90.0 1.3 %copy.55 = f32[2,1,48,4,288]{4,2,3,0,1:T(8,128)} copy(f32[2,1,48,4,288]{2,0,4,3,1:T(2,128)S(1)} %bitcast.39) | data formatting | bytes 884736 | tf_op jit(solution)/shard_map/all_to_all | solution.py:129
  91.4 1.5 %reshape.589 = f32[2,4,13824]{2,1,0:T(4,128)S(1)} reshape(f32[2,4,1,48,288]{4,3,1,0,2:T(8,128)} %bitcast.48) | data formatting | bytes 884736 | tf_op jit(solution)/shard_map/reshape | solution.py:105
  93.0 0.4 multiply_multiply_fusion.4
  93.5 0.7 multiply_multiply_fusion.3
  94.2 0.4 multiply_multiply_fusion.2
  94.7 0.7 multiply_multiply_fusion.1
  95.5 0.4 multiply_multiply_fusion
  95.9 0.8 copy-done.4
  96.7 1.3 %add_subtract_fusion = f32[2,4,13824]{2,1,0:T(4,128)} fusion(f32[2,3,13824]{2,1,0:T(4,128)S(1)} %bitcast.52, f32[2,4,13824]{2,1,0:T(4,128)S(1)} %get-tuple-element.7, f32[2,3,13824]{2,1,0:T(4,128)S(1)} %bitcast.46, f32[2,4,13824]{2,1,0:T(4,128)S(1)} %reshape.590), kind=kLoop, calls=%fused_computation.205 | loop fusion | flops 1327104 | bytes 1990656 | tf_op jit(solution)/shard_map/sub | solution.py:96
  98.0 2.3 %reshape.591 = f32[2,4,48,288]{3,2,1,0:T(8,128)} reshape(f32[2,4,13824]{2,1,0:T(4,128)} %add_subtract_fusion) | data formatting | bytes 884736 | tf_op jit(solution)/shard_map/reshape | solution.py:107
  100.3 1.1 copy.58
  101.4 11.9 %all_to_all.48 = f32[2,4,48,288]{3,2,0,1:T(8,128)S(1)} all-to-all(f32[2,4,48,288]{3,2,0,1:T(8,128)S(1)} %copy.58), channel_id=1, replica_groups=mesh['lat'=8,'lev'=4] {'lev'}, dimensions={1} | all-to-all | bytes 884736 | tf_op jit(solution)/shard_map/all_to_all | solution.py:106
  113.3 1.2 copy.59
  114.5 1.4 %all_to_all.44 = f32[2,1,48,1152]{3,2,1,0:T(8,128)S(1)} reshape(f32[2,1,48,4,288]{4,3,2,0,1:T(4,128)} %copy.59) | data formatting | bytes 884736 | tf_op jit(solution)/shard_map/all_to_all | solution.py:106
  116.2 0.5 fusion.129
  117.0 0.5 fusion.69
  117.7 4.5 %collective-permute-start.9 = (f32[2,1,3,1152]{3,2,1,0:T(4,128)S(1)}, f32[2,1,3,1152]{3,2,1,0:T(4,128)S(1)}, u32[]{:S(2)}, u32[]{:S(2)}) collective-permute-start(f32[2,1,3,1152]{3,2,1,0:T(4,128)S(1)} %get-tuple-element.30), channel_id=1, source_target_pairs={{0,4},{4,8},{8,12},{12,16},{16,20},{20,24},{24,28},{1,5},{5,9},{9,... | collective-permute-start | bytes 82952 | tf_op jit(solution)/shard_map/ppermute | solution.py:21
  122.2 1.3 collective-permute-start.10
  123.5 2.3 %fusion.142 = f32[2,13824]{1,0:T(2,128)S(1)} fusion(f32[2,4,13824]{2,1,0:T(4,128)} %copy-done.4, f32[2,4,13824]{2,1,0:T(4,128)} %copy-done, f32[2,4,13824]{2,1,0:T(4,128)} %copy-done.3, f32[2,4,13824]{2,1,0:T(4,128)S(1)} %get-tuple-element.8, f32[2,4,13824]{2,1,0:T(4,128)} %copy-done.2, f32[2,4,13824]{2,1,0:T(4,128)S(1)} %multiply_multiply_fusion.5), kind=kLoop, calls=%fused_computation.228 | loop fusion | flops 138240 | bytes 774144 | tf_op jit(solution)/shard_map/add | solution.py:97
  125.8 0.8 reshape.592
  126.7 1.4 %collective-permute-done.10 = f32[2,1,3,1152]{3,2,1,0:T(4,128)S(1)} collective-permute-done((f32[2,1,3,1152]{3,2,1,0:T(4,128)S(1)}, f32[2,1,3,1152]{3,2,1,0:T(4,128)S(1)}, u32[]{:S(2)}, u32[]{:S(2)}) %collective-permute-start.10) | collective-permute-done | bytes 27680 | tf_op jit(solution)/shard_map/ppermute | solution.py:24
  128.9 0.8 fusion.130
  (74 shorter events, 9.1 us)
Async XLA Ops:
  0.6 9.1 %copy-start.5 = (f32[1,48,1152]{2,1,0:T(8,128)S(1)}, f32[1,48,1152]{2,1,0:T(8,128)}, u32[]{:S(2)}) copy-start(f32[1,48,1152]{2,1,0:T(8,128)} %param.5) | copy-start | bytes 663556
  0.6 9.0 %copy-start.1 = (f32[2,1,48,1152]{3,2,1,0:T(8,128)S(1)}, f32[2,1,48,1152]{3,2,1,0:T(8,128)}, u32[]{:S(2)}) copy-start(f32[2,1,48,1152]{3,2,1,0:T(8,128)} %param.4) | copy-start | bytes 1327108
  1.8 14.7 %collective-permute-start = (f32[1,1,1152]{2,1,0:T(1,128)S(1)}, f32[1,1,1152]{2,1,0:T(1,128)S(1)}, u32[]{:S(2)}, u32[]{:S(2)}) collective-permute-start(f32[1,1,1152]{2,1,0:T(1,128)S(1)} %slice.702), channel_id=1, source_target_pairs={{0,4},{4,8},{8,12},{12,16},{16,20},{20,24},{24,28},{1,5},{5,9},{9,... | collective-permute-start | bytes 13832 | tf_op jit(solution)/shard_map/ppermute | solution.py:13
  11.4 5.0 %copy-start.6 = (f32[1,48,1152]{2,1,0:T(8,128)S(1)}, f32[1,48,1152]{2,1,0:T(8,128)}, u32[]{:S(2)}) copy-start(f32[1,48,1152]{2,1,0:T(8,128)} %param.6) | copy-start | bytes 663556
  11.7 5.1 %collective-permute-start.1 = (f32[2,1,3,1152]{3,2,1,0:T(4,128)S(1)}, f32[2,1,3,1152]{3,2,1,0:T(4,128)S(1)}, u32[]{:S(2)}, u32[]{:S(2)}) collective-permute-start(f32[2,1,3,1152]{3,2,1,0:T(4,128)S(1)} %get-tuple-element.46), channel_id=1, source_target_pairs={{0,4},{4,8},{8,12},{12,16},{16,20},{20,24},{24,28},{1,5},{5,9},{9,... | collective-permute-start | bytes 82952 | tf_op jit(solution)/shard_map/ppermute | solution.py:21
  15.1 5.9 %collective-permute-start.2 = (f32[2,1,3,1152]{3,2,1,0:T(4,128)S(1)}, f32[2,1,3,1152]{3,2,1,0:T(4,128)S(1)}, u32[]{:S(2)}, u32[]{:S(2)}) collective-permute-start(f32[2,1,3,1152]{3,2,1,0:T(4,128)S(1)} %get-tuple-element.47), channel_id=1, source_target_pairs={{4,0},{8,4},{12,8},{16,12},{20,16},{24,20},{28,24},{5,1},{9,5},{13... | collective-permute-start | bytes 82952 | tf_op jit(solution)/shard_map/ppermute | solution.py:24
  23.7 6.0 %collective-permute-start.3 = (f32[2,1,3,1152]{3,2,1,0:T(4,128)S(1)}, f32[2,1,3,1152]{3,2,1,0:T(4,128)S(1)}, u32[]{:S(2)}, u32[]{:S(2)}) collective-permute-start(f32[2,1,3,1152]{3,2,1,0:T(4,128)S(1)} %get-tuple-element.42), channel_id=1, source_target_pairs={{0,4},{4,8},{8,12},{12,16},{16,20},{20,24},{24,28},{1,5},{5,9},{9,... | collective-permute-start | bytes 82952 | tf_op jit(solution)/shard_map/ppermute | solution.py:21
  28.0 5.9 %collective-permute-start.4 = (f32[2,1,3,1152]{3,2,1,0:T(4,128)S(1)}, f32[2,1,3,1152]{3,2,1,0:T(4,128)S(1)}, u32[]{:S(2)}, u32[]{:S(2)}) collective-permute-start(f32[2,1,3,1152]{3,2,1,0:T(4,128)S(1)} %get-tuple-element.43), channel_id=1, source_target_pairs={{4,0},{8,4},{12,8},{16,12},{20,16},{24,20},{28,24},{5,1},{9,5},{13... | collective-permute-start | bytes 82952 | tf_op jit(solution)/shard_map/ppermute | solution.py:24
  36.6 5.2 %collective-permute-start.5 = (f32[2,1,3,1152]{3,2,1,0:T(4,128)S(1)}, f32[2,1,3,1152]{3,2,1,0:T(4,128)S(1)}, u32[]{:S(2)}, u32[]{:S(2)}) collective-permute-start(f32[2,1,3,1152]{3,2,1,0:T(4,128)S(1)} %get-tuple-element.38), channel_id=1, source_target_pairs={{0,4},{4,8},{8,12},{12,16},{16,20},{20,24},{24,28},{1,5},{5,9},{9,... | collective-permute-start | bytes 82952 | tf_op jit(solution)/shard_map/ppermute | solution.py:21
  40.0 5.9 %collective-permute-start.6 = (f32[2,1,3,1152]{3,2,1,0:T(4,128)S(1)}, f32[2,1,3,1152]{3,2,1,0:T(4,128)S(1)}, u32[]{:S(2)}, u32[]{:S(2)}) collective-permute-start(f32[2,1,3,1152]{3,2,1,0:T(4,128)S(1)} %get-tuple-element.39), channel_id=1, source_target_pairs={{4,0},{8,4},{12,8},{16,12},{20,16},{24,20},{28,24},{5,1},{9,5},{13... | collective-permute-start | bytes 82952 | tf_op jit(solution)/shard_map/ppermute | solution.py:24
  48.6 14.8 %collective-permute-start.7 = (f32[2,1,3,1152]{3,2,1,0:T(4,128)S(1)}, f32[2,1,3,1152]{3,2,1,0:T(4,128)S(1)}, u32[]{:S(2)}, u32[]{:S(2)}) collective-permute-start(f32[2,1,3,1152]{3,2,1,0:T(4,128)S(1)} %get-tuple-element.34), channel_id=1, source_target_pairs={{0,4},{4,8},{8,12},{12,16},{16,20},{20,24},{24,28},{1,5},{5,9},{9,... | collective-permute-start | bytes 82952 | tf_op jit(solution)/shard_map/ppermute | solution.py:21
  52.9 10.5 %collective-permute-start.8 = (f32[2,1,3,1152]{3,2,1,0:T(4,128)S(1)}, f32[2,1,3,1152]{3,2,1,0:T(4,128)S(1)}, u32[]{:S(2)}, u32[]{:S(2)}) collective-permute-start(f32[2,1,3,1152]{3,2,1,0:T(4,128)S(1)} %get-tuple-element.35), channel_id=1, source_target_pairs={{4,0},{8,4},{12,8},{16,12},{20,16},{24,20},{28,24},{5,1},{9,5},{13... | collective-permute-start | bytes 82952 | tf_op jit(solution)/shard_map/ppermute | solution.py:24
  59.3 12.1 %all-to-all-start.1 = ((f32[4,1,27648]{2,1,0:T(1,128)}), f32[4,1,27648]{2,1,0:T(1,128)}, u32[]{:S(2)}, u32[]{:S(2)}) async-start(f32[4,1,27648]{2,1,0:T(1,128)} %reshape.594), calls=%async_computation.1 | async-start | bytes 884736 | tf_op jit(solution)/shard_map/all_to_all | solution.py:130
  71.4 12.1 %all-to-all-start = ((f32[4,1,27648]{2,1,0:T(1,128)}), f32[4,1,27648]{2,1,0:T(1,128)}, u32[]{:S(2)}, u32[]{:S(2)}) async-start(f32[4,1,27648]{2,1,0:T(1,128)} %reshape.596), calls=%async_computation | async-start | bytes 884736 | tf_op jit(solution)/shard_map/all_to_all | solution.py:129
  93.5 0.8 copy-start.2
  94.7 0.8 copy-start.3
  95.5 2.6 %copy-start = (f32[2,4,13824]{2,1,0:T(4,128)}, f32[2,4,13824]{2,1,0:T(4,128)S(1)}, u32[]{:S(2)}) copy-start(f32[2,4,13824]{2,1,0:T(4,128)S(1)} %get-tuple-element.6) | copy-start | bytes 1327108
  95.9 0.8 copy-start.4
  117.7 9.0 %collective-permute-start.9 = (f32[2,1,3,1152]{3,2,1,0:T(4,128)S(1)}, f32[2,1,3,1152]{3,2,1,0:T(4,128)S(1)}, u32[]{:S(2)}, u32[]{:S(2)}) collective-permute-start(f32[2,1,3,1152]{3,2,1,0:T(4,128)S(1)} %get-tuple-element.30), channel_id=1, source_target_pairs={{0,4},{4,8},{8,12},{12,16},{16,20},{20,24},{24,28},{1,5},{5,9},{9,... | collective-permute-start | bytes 82952 | tf_op jit(solution)/shard_map/ppermute | solution.py:21
  122.2 5.9 %collective-permute-start.10 = (f32[2,1,3,1152]{3,2,1,0:T(4,128)S(1)}, f32[2,1,3,1152]{3,2,1,0:T(4,128)S(1)}, u32[]{:S(2)}, u32[]{:S(2)}) collective-permute-start(f32[2,1,3,1152]{3,2,1,0:T(4,128)S(1)} %get-tuple-element.31), channel_id=1, source_target_pairs={{4,0},{8,4},{12,8},{16,12},{20,16},{24,20},{28,24},{5,1},{9,5},{13... | collective-permute-start | bytes 82952 | tf_op jit(solution)/shard_map/ppermute | solution.py:24
where the time goes:
time: 131 us; the launch traced here: 130 us
  starting transfers between devices  39.9 us (30%)
  other arithmetic  28.9 us (22%)
  local copies, waits for them, and re-layouts  28.2 us (22%)
  waiting for transfers between devices  19.6 us (15%)
  blocking collectives  11.9 us (9%)
    ppermute x5, starting transfers between devices, extended(): lax.ppermute(lax.slice_in_dim(block, block.shape[dim] - width, None, axis...  20.1 us
    ppermute x5, waiting for transfers between devices, extended(): lax.ppermute(lax.slice_in_dim(block, 0, width, axis=dim), axis, backward)  14 us
    unnamed x19, local copies, waits for them, and re-layouts  13.3 us
    all_to_all x1, blocking collectives, columns_settle(): lax.all_to_all(settled.reshape(shape_full), 'lev', split_axis=1, concat_a...  11.9 us
    ppermute x5, starting transfers between devices, extended(): lax.ppermute(lax.slice_in_dim(block, 0, width, axis=dim), axis, backward)  6.64 us
    ppermute x1, starting transfers between devices, passed_along(): return lax.ppermute(block, axis, route)  4.9 us
    all_to_all x1, starting transfers between devices, on_device(): lax.all_to_all(fall_speed, 'lev', split_axis=3, concat_axis=1, tiled=True)  4.13 us
    all_to_all x1, starting transfers between devices, on_device(): lax.all_to_all(field, 'lev', split_axis=3, concat_axis=1, tiled=True)  4.12 us
  transfers between devices with their start and end apart: 13, of which 8 were waited for; matrix products, arithmetic and copies ran while one was open for 19% of the time, Pallas kernels for 0%

commit v1 on v0

--- a/solution.py
+++ b/solution.py
@@ -127,7 +127,12 @@
     field, deposit = columns_settle(
         (
             lax.all_to_all(field, "lev", split_axis=3, concat_axis=1, tiled=True),
-            lax.all_to_all(fall_speed, "lev", split_axis=3, concat_axis=1, tiled=True),
+            jnp.concatenate(
+                lax.all_to_all(
+                    jnp.stack(jnp.split(fall_speed, lax.axis_size("lev"), axis=3)), "lev", 0, 0
+                ),
+                axis=1,
+            ),
         )
     )
     field = zonal(field, east_courant)

time: 131 us -> 127 us (0.969)
  local copies, waits for them, and re-layouts: 28.2 us -> 22.9 us
  waiting for transfers between devices: 19.6 us -> 24.7 us
  other arithmetic: 28.9 us -> 26.2 us
    unnamed x19 -> x20, local copies, waits for them, and re-layouts: 13.3 us -> 6.64 us
    all_to_all x1, waiting for transfers between devices: 1.67 us -> 6.28 us  [on_device(): lax.all_to_all(field, 'lev', split_axis=3, concat_axis=1, tiled=True)]
    all_to_all x1 -> x0, other arithmetic: 2.81 us -> none  [on_device(): lax.all_to_all(fall_speed, 'lev', split_axis=3, concat_axis=1, tiled=True)]
    another operation x0 -> x3, local copies, waits for them, and re-layouts: none -> 2.52 us  [the longest x1 1.62 us: columns_settle(): speed_piece.reshape(flat_shape)]
    all_to_all x1, waiting for transfers between devices: 3.09 us -> 4.5 us  [on_device(): lax.all_to_all(jnp.stack(jnp.split(fall_speed, lax.axis_size('lev'), axis...]
  transfers between devices with their start and end apart: 13 -> 13, of which waited for: 8 -> 7; matrix products, arithmetic and copies ran while one was open for 19% -> 13% of each run, Pallas kernels for 0% -> 0%
where the time goes in v1:
time: 127 us; the launch traced here: 126 us
  starting transfers between devices  39.2 us (31%)
  other arithmetic  26.2 us (21%)
  waiting for transfers between devices  24.7 us (19%)
  local copies, waits for them, and re-layouts  22.9 us (18%)
  blocking collectives  11.9 us (9%)
  between operations  1.29 us (1%)
    ppermute x5, starting transfers between devices, extended(): lax.ppermute(lax.slice_in_dim(block, block.shape[dim] - width, None, axis...  20.1 us
    ppermute x5, waiting for transfers between devices, extended(): lax.ppermute(lax.slice_in_dim(block, 0, width, axis=dim), axis, backward)  13.8 us
    all_to_all x1, blocking collectives, columns_settle(): lax.all_to_all(settled.reshape(shape_full), 'lev', split_axis=1, concat_a...  11.9 us
    unnamed x20, local copies, waits for them, and re-layouts  6.64 us
    ppermute x5, starting transfers between devices, extended(): lax.ppermute(lax.slice_in_dim(block, 0, width, axis=dim), axis, backward)  6.46 us
    all_to_all x1, waiting for transfers between devices, on_device(): lax.all_to_all(field, 'lev', split_axis=3, concat_axis=1, tiled=True)  6.28 us
    ppermute x1, starting transfers between devices, passed_along(): return lax.ppermute(block, axis, route)  4.9 us
    all_to_all x1, waiting for transfers between devices, on_device(): lax.all_to_all(jnp.stack(jnp.split(fall_speed, lax.axis_size('lev'), axis...  4.5 us
  transfers between devices with their start and end apart: 13, of which 7 were waited for; matrix products, arithmetic and copies ran while one was open for 13% of the time, Pallas kernels for 0%

profile of v1, /device:TPU:0, one launch (start us, length us, event | category | flops | bytes accessed | tf_op | source)
XLA Modules:
  0.0 126.3 jit_solution(12682020555665694493)
XLA Ops:
  0.7 1.1 broadcast_select_fusion
  1.8 4.9 %collective-permute-start = (f32[1,1,1152]{2,1,0:T(1,128)S(1)}, f32[1,1,1152]{2,1,0:T(1,128)S(1)}, u32[]{:S(2)}, u32[]{:S(2)}) collective-permute-start(f32[1,1,1152]{2,1,0:T(1,128)S(1)} %slice.702), channel_id=1, source_target_pairs={{0,4},{4,8},{8,12},{12,16},{16,20},{20,24},{24,28},{1,5},{5,9},{9,... | collective-permute-start | bytes 13832 | tf_op jit(solution)/shard_map/ppermute | solution.py:13
  6.7 0.8 fusion.153
  7.5 1.1 fusion.141
  8.6 1.1 abs_multiply_fusion.1
  10.2 0.5 fusion.113
  10.6 0.3 slice_subtract_fusion.9
  11.0 0.5 fusion.105
  11.7 3.4 %collective-permute-start.1 = (f32[2,1,3,1152]{3,2,1,0:T(4,128)S(1)}, f32[2,1,3,1152]{3,2,1,0:T(4,128)S(1)}, u32[]{:S(2)}, u32[]{:S(2)}) collective-permute-start(f32[2,1,3,1152]{3,2,1,0:T(4,128)S(1)} %get-tuple-element.46), channel_id=1, source_target_pairs={{0,4},{4,8},{8,12},{12,16},{16,20},{20,24},{24,28},{1,5},{5,9},{9,... | collective-permute-start | bytes 82952 | tf_op jit(solution)/shard_map/ppermute | solution.py:21
  15.1 1.3 %collective-permute-start.2 = (f32[2,1,3,1152]{3,2,1,0:T(4,128)S(1)}, f32[2,1,3,1152]{3,2,1,0:T(4,128)S(1)}, u32[]{:S(2)}, u32[]{:S(2)}) collective-permute-start(f32[2,1,3,1152]{3,2,1,0:T(4,128)S(1)} %get-tuple-element.47), channel_id=1, source_target_pairs={{4,0},{8,4},{12,8},{16,12},{20,16},{24,20},{28,24},{5,1},{9,5},{13... | collective-permute-start | bytes 82952 | tf_op jit(solution)/shard_map/ppermute | solution.py:24
  16.8 4.2 %collective-permute-done.2 = f32[2,1,3,1152]{3,2,1,0:T(4,128)S(1)} collective-permute-done((f32[2,1,3,1152]{3,2,1,0:T(4,128)S(1)}, f32[2,1,3,1152]{3,2,1,0:T(4,128)S(1)}, u32[]{:S(2)}, u32[]{:S(2)}) %collective-permute-start.2) | collective-permute-done | bytes 27680 | tf_op jit(solution)/shard_map/ppermute | solution.py:24
  21.5 0.3 fusion.40
  22.2 0.5 fusion.117
  22.7 0.3 slice_subtract_fusion.8
  23.0 0.5 fusion.96
  23.8 4.3 %collective-permute-start.3 = (f32[2,1,3,1152]{3,2,1,0:T(4,128)S(1)}, f32[2,1,3,1152]{3,2,1,0:T(4,128)S(1)}, u32[]{:S(2)}, u32[]{:S(2)}) collective-permute-start(f32[2,1,3,1152]{3,2,1,0:T(4,128)S(1)} %get-tuple-element.42), channel_id=1, source_target_pairs={{0,4},{4,8},{8,12},{12,16},{16,20},{20,24},{24,28},{1,5},{5,9},{9,... | collective-permute-start | bytes 82952 | tf_op jit(solution)/shard_map/ppermute | solution.py:21
  28.1 1.3 %collective-permute-start.4 = (f32[2,1,3,1152]{3,2,1,0:T(4,128)S(1)}, f32[2,1,3,1152]{3,2,1,0:T(4,128)S(1)}, u32[]{:S(2)}, u32[]{:S(2)}) collective-permute-start(f32[2,1,3,1152]{3,2,1,0:T(4,128)S(1)} %get-tuple-element.43), channel_id=1, source_target_pairs={{4,0},{8,4},{12,8},{16,12},{20,16},{24,20},{28,24},{5,1},{9,5},{13... | collective-permute-start | bytes 82952 | tf_op jit(solution)/shard_map/ppermute | solution.py:24
  29.7 4.2 %collective-permute-done.4 = f32[2,1,3,1152]{3,2,1,0:T(4,128)S(1)} collective-permute-done((f32[2,1,3,1152]{3,2,1,0:T(4,128)S(1)}, f32[2,1,3,1152]{3,2,1,0:T(4,128)S(1)}, u32[]{:S(2)}, u32[]{:S(2)}) %collective-permute-start.4) | collective-permute-done | bytes 27680 | tf_op jit(solution)/shard_map/ppermute | solution.py:24
  35.2 0.5 fusion.121
  35.6 0.3 slice_subtract_fusion.7
  36.0 0.5 fusion.87
  36.7 3.4 %collective-permute-start.5 = (f32[2,1,3,1152]{3,2,1,0:T(4,128)S(1)}, f32[2,1,3,1152]{3,2,1,0:T(4,128)S(1)}, u32[]{:S(2)}, u32[]{:S(2)}) collective-permute-start(f32[2,1,3,1152]{3,2,1,0:T(4,128)S(1)} %get-tuple-element.38), channel_id=1, source_target_pairs={{0,4},{4,8},{8,12},{12,16},{16,20},{20,24},{24,28},{1,5},{5,9},{9,... | collective-permute-start | bytes 82952 | tf_op jit(solution)/shard_map/ppermute | solution.py:21
  40.1 1.3 %collective-permute-start.6 = (f32[2,1,3,1152]{3,2,1,0:T(4,128)S(1)}, f32[2,1,3,1152]{3,2,1,0:T(4,128)S(1)}, u32[]{:S(2)}, u32[]{:S(2)}) collective-permute-start(f32[2,1,3,1152]{3,2,1,0:T(4,128)S(1)} %get-tuple-element.39), channel_id=1, source_target_pairs={{4,0},{8,4},{12,8},{16,12},{20,16},{24,20},{28,24},{5,1},{9,5},{13... | collective-permute-start | bytes 82952 | tf_op jit(solution)/shard_map/ppermute | solution.py:24
  41.4 0.8 slice_bitcast_fusion.3
  42.2 3.8 %collective-permute-done.6 = f32[2,1,3,1152]{3,2,1,0:T(4,128)S(1)} collective-permute-done((f32[2,1,3,1152]{3,2,1,0:T(4,128)S(1)}, f32[2,1,3,1152]{3,2,1,0:T(4,128)S(1)}, u32[]{:S(2)}, u32[]{:S(2)}) %collective-permute-start.6) | collective-permute-done | bytes 27680 | tf_op jit(solution)/shard_map/ppermute | solution.py:24
  47.2 0.5 fusion.125
  47.7 0.3 slice_subtract_fusion.6
  48.0 0.5 fusion.78
  48.7 4.3 %collective-permute-start.7 = (f32[2,1,3,1152]{3,2,1,0:T(4,128)S(1)}, f32[2,1,3,1152]{3,2,1,0:T(4,128)S(1)}, u32[]{:S(2)}, u32[]{:S(2)}) collective-permute-start(f32[2,1,3,1152]{3,2,1,0:T(4,128)S(1)} %get-tuple-element.34), channel_id=1, source_target_pairs={{0,4},{4,8},{8,12},{12,16},{16,20},{20,24},{24,28},{1,5},{5,9},{9,... | collective-permute-start | bytes 82952 | tf_op jit(solution)/shard_map/ppermute | solution.py:21
  53.1 1.3 %collective-permute-start.8 = (f32[2,1,3,1152]{3,2,1,0:T(4,128)S(1)}, f32[2,1,3,1152]{3,2,1,0:T(4,128)S(1)}, u32[]{:S(2)}, u32[]{:S(2)}) collective-permute-start(f32[2,1,3,1152]{3,2,1,0:T(4,128)S(1)} %get-tuple-element.35), channel_id=1, source_target_pairs={{4,0},{8,4},{12,8},{16,12},{20,16},{24,20},{28,24},{5,1},{9,5},{13... | collective-permute-start | bytes 82952 | tf_op jit(solution)/shard_map/ppermute | solution.py:24
  54.4 0.9 pad_maximum_fusion
  55.3 4.3 %all-to-all-start.1 = ((f32[4,2,1,48,288]{4,3,1,2,0:T(8,128)}), f32[4,2,1,48,288]{4,3,1,2,0:T(8,128)}, u32[]{:S(2)}, u32[]{:S(2)}) async-start(f32[4,2,1,48,288]{4,3,1,2,0:T(8,128)} %pad_maximum_fusion), calls=%async_computation.1 | async-start | bytes 1179648 | tf_op jit(solution)/shard_map/all_to_all | solution.py:131
  60.5 1.1 copy.62
  61.6 2.8 %reshape.594 = f32[4,1,27648]{2,1,0:T(1,128)} reshape(f32[1152,1,2,48]{3,2,1,0:T(2,128)S(1)} %bitcast.43) | data formatting | bytes 884736
  64.5 4.5 %all-to-all-done.1 = f32[4,2,1,48,288]{4,3,1,2,0:T(8,128)} async-done(((f32[4,2,1,48,288]{4,3,1,2,0:T(8,128)}), f32[4,2,1,48,288]{4,3,1,2,0:T(8,128)}, u32[]{:S(2)}, u32[]{:S(2)}) %all-to-all-start.1) | async-done | bytes 442400 | tf_op jit(solution)/shard_map/all_to_all | solution.py:131
  69.0 3.5 %all-to-all-start = ((f32[4,1,27648]{2,1,0:T(1,128)}), f32[4,1,27648]{2,1,0:T(1,128)S(1)}, u32[]{:S(2)}, u32[]{:S(2)}) async-start(f32[4,1,27648]{2,1,0:T(1,128)} %reshape.594), calls=%async_computation | async-start | bytes 884736 | tf_op jit(solution)/shard_map/all_to_all | solution.py:129
  72.5 1.6 %reshape.592 = f32[2,4,13824]{2,0,1:T(2,128)S(1)} reshape(f32[2,4,1,48,288]{4,3,0,2,1:T(8,128)} %bitcast.13) | data formatting | bytes 884736 | tf_op jit(solution)/shard_map/reshape;reshape | solution.py:105
  74.1 6.3 %all-to-all-done = f32[4,1,27648]{2,1,0:T(1,128)S(1)} async-done(((f32[4,1,27648]{2,1,0:T(1,128)}), f32[4,1,27648]{2,1,0:T(1,128)S(1)}, u32[]{:S(2)}, u32[]{:S(2)}) %all-to-all-start) | async-done | bytes 442400 | tf_op jit(solution)/shard_map/all_to_all | solution.py:129
  80.4 0.5 broadcast.305
  80.9 2.7 %reduce.2 = f32[4,27648]{1,0:T(4,128)} reduce(f32[4,1,27648]{2,1,0:T(1,128)S(1)} %all-to-all-done, f32[]{:T(128)} %broadcast.305), dimensions={1}, to_apply=%all_to_all.27.reduce_sub_computation | reduce | bytes 884740 | tf_op jit(solution)/shard_map/all_to_all | solution.py:129
  83.6 2.9 %reshape.595 = f32[1152,1,2,48]{3,2,1,0:T(2,128)S(1)} reshape(f32[4,27648]{1,0:T(4,128)} %reduce.2) | data formatting | bytes 884736
  86.5 1.3 %copy.63 = f32[2,1,48,4,288]{4,2,3,0,1:T(8,128)} copy(f32[2,1,48,4,288]{2,0,4,3,1:T(2,128)S(1)} %bitcast.44) | data formatting | bytes 884736 | tf_op jit(solution)/shard_map/all_to_all | solution.py:129
  87.8 1.5 %reshape.588 = f32[2,4,13824]{2,1,0:T(4,128)S(1)} reshape(f32[2,4,1,48,288]{4,3,1,0,2:T(8,128)} %bitcast.51) | data formatting | bytes 884736 | tf_op jit(solution)/shard_map/reshape | solution.py:105
  89.5 0.4 multiply_multiply_fusion.4
  90.0 0.7 multiply_multiply_fusion.3
  90.7 0.4 multiply_multiply_fusion.2
  91.2 0.7 multiply_multiply_fusion.1
  91.9 0.4 multiply_multiply_fusion
  92.4 0.8 copy-done.4
  93.2 1.3 %add_subtract_fusion = f32[2,4,13824]{2,1,0:T(4,128)} fusion(f32[2,3,13824]{2,1,0:T(4,128)S(1)} %bitcast.55, f32[2,4,13824]{2,1,0:T(4,128)S(1)} %get-tuple-element.7, f32[2,3,13824]{2,1,0:T(4,128)S(1)} %bitcast.50, f32[2,4,13824]{2,0,1:T(2,128)S(1)} %reshape.592), kind=kLoop, calls=%fused_computation.206 | loop fusion | flops 1327104 | bytes 1990656 | tf_op jit(solution)/shard_map/sub | solution.py:96
  94.5 2.3 %reshape.590 = f32[2,4,48,288]{3,2,1,0:T(8,128)} reshape(f32[2,4,13824]{2,1,0:T(4,128)} %add_subtract_fusion) | data formatting | bytes 884736 | tf_op jit(solution)/shard_map/reshape | solution.py:107
  96.8 1.1 copy.68
  97.9 11.9 %all_to_all.38 = f32[2,4,48,288]{3,2,0,1:T(8,128)S(1)} all-to-all(f32[2,4,48,288]{3,2,0,1:T(8,128)S(1)} %copy.68), channel_id=1, replica_groups=mesh['lat'=8,'lev'=4] {'lev'}, dimensions={1} | all-to-all | bytes 884736 | tf_op jit(solution)/shard_map/all_to_all | solution.py:106
  109.8 1.2 copy.69
  111.0 1.4 %all_to_all.34 = f32[2,1,48,1152]{3,2,1,0:T(8,128)S(1)} reshape(f32[2,1,48,4,288]{4,3,2,0,1:T(4,128)} %copy.69) | data formatting | bytes 884736 | tf_op jit(solution)/shard_map/all_to_all | solution.py:106
  112.7 0.5 fusion.129
  113.2 0.3 slice_subtract_fusion.5
  113.5 0.5 fusion.69
  114.2 4.5 %collective-permute-start.9 = (f32[2,1,3,1152]{3,2,1,0:T(4,128)S(1)}, f32[2,1,3,1152]{3,2,1,0:T(4,128)S(1)}, u32[]{:S(2)}, u32[]{:S(2)}) collective-permute-start(f32[2,1,3,1152]{3,2,1,0:T(4,128)S(1)} %get-tuple-element.30), channel_id=1, source_target_pairs={{0,4},{4,8},{8,12},{12,16},{16,20},{20,24},{24,28},{1,5},{5,9},{9,... | collective-permute-start | bytes 82952 | tf_op jit(solution)/shard_map/ppermute | solution.py:21
  118.8 1.3 %collective-permute-start.10 = (f32[2,1,3,1152]{3,2,1,0:T(4,128)S(1)}, f32[2,1,3,1152]{3,2,1,0:T(4,128)S(1)}, u32[]{:S(2)}, u32[]{:S(2)}) collective-permute-start(f32[2,1,3,1152]{3,2,1,0:T(4,128)S(1)} %get-tuple-element.31), channel_id=1, source_target_pairs={{4,0},{8,4},{12,8},{16,12},{20,16},{24,20},{28,24},{5,1},{9,5},{13... | collective-permute-start | bytes 82952 | tf_op jit(solution)/shard_map/ppermute | solution.py:24
  120.1 2.2 %fusion.142 = f32[2,13824]{1,0:T(2,128)S(1)} fusion(f32[2,4,13824]{2,1,0:T(4,128)} %copy-done.4, f32[2,4,13824]{2,1,0:T(4,128)} %copy-done, f32[2,4,13824]{2,1,0:T(4,128)} %copy-done.3, f32[2,4,13824]{2,1,0:T(4,128)S(1)} %get-tuple-element.8, f32[2,4,13824]{2,1,0:T(4,128)} %copy-done.2, f32[2,4,13824]{2,1,0:T(4,128)S(1)} %multiply_multiply_fusion.5), kind=kLoop, calls=%fused_computation.233 | loop fusion | flops 138240 | bytes 774144 | tf_op jit(solution)/shard_map/add | solution.py:97
  122.3 0.8 reshape.591
  123.1 1.5 %collective-permute-done.10 = f32[2,1,3,1152]{3,2,1,0:T(4,128)S(1)} collective-permute-done((f32[2,1,3,1152]{3,2,1,0:T(4,128)S(1)}, f32[2,1,3,1152]{3,2,1,0:T(4,128)S(1)}, u32[]{:S(2)}, u32[]{:S(2)}) %collective-permute-start.10) | collective-permute-done | bytes 27680 | tf_op jit(solution)/shard_map/ppermute | solution.py:24
  125.5 0.8 fusion.130
  (76 shorter events, 7.7 us)
Async XLA Ops:
  0.6 9.1 %copy-start.5 = (f32[1,48,1152]{2,1,0:T(8,128)S(1)}, f32[1,48,1152]{2,1,0:T(8,128)}, u32[]{:S(2)}) copy-start(f32[1,48,1152]{2,1,0:T(8,128)} %param.5) | copy-start | bytes 663556
  0.6 9.0 %copy-start.1 = (f32[2,1,48,1152]{3,2,1,0:T(8,128)S(1)}, f32[2,1,48,1152]{3,2,1,0:T(8,128)}, u32[]{:S(2)}) copy-start(f32[2,1,48,1152]{3,2,1,0:T(8,128)} %param.4) | copy-start | bytes 1327108
  1.8 14.8 %collective-permute-start = (f32[1,1,1152]{2,1,0:T(1,128)S(1)}, f32[1,1,1152]{2,1,0:T(1,128)S(1)}, u32[]{:S(2)}, u32[]{:S(2)}) collective-permute-start(f32[1,1,1152]{2,1,0:T(1,128)S(1)} %slice.702), channel_id=1, source_target_pairs={{0,4},{4,8},{8,12},{12,16},{16,20},{20,24},{24,28},{1,5},{5,9},{9,... | collective-permute-start | bytes 13832 | tf_op jit(solution)/shard_map/ppermute | solution.py:13
  11.5 5.0 %copy-start.6 = (f32[1,48,1152]{2,1,0:T(8,128)S(1)}, f32[1,48,1152]{2,1,0:T(8,128)}, u32[]{:S(2)}) copy-start(f32[1,48,1152]{2,1,0:T(8,128)} %param.6) | copy-start | bytes 663556
  11.7 5.1 %collective-permute-start.1 = (f32[2,1,3,1152]{3,2,1,0:T(4,128)S(1)}, f32[2,1,3,1152]{3,2,1,0:T(4,128)S(1)}, u32[]{:S(2)}, u32[]{:S(2)}) collective-permute-start(f32[2,1,3,1152]{3,2,1,0:T(4,128)S(1)} %get-tuple-element.46), channel_id=1, source_target_pairs={{0,4},{4,8},{8,12},{12,16},{16,20},{20,24},{24,28},{1,5},{5,9},{9,... | collective-permute-start | bytes 82952 | tf_op jit(solution)/shard_map/ppermute | solution.py:21
  15.1 5.9 %collective-permute-start.2 = (f32[2,1,3,1152]{3,2,1,0:T(4,128)S(1)}, f32[2,1,3,1152]{3,2,1,0:T(4,128)S(1)}, u32[]{:S(2)}, u32[]{:S(2)}) collective-permute-start(f32[2,1,3,1152]{3,2,1,0:T(4,128)S(1)} %get-tuple-element.47), channel_id=1, source_target_pairs={{4,0},{8,4},{12,8},{16,12},{20,16},{24,20},{28,24},{5,1},{9,5},{13... | collective-permute-start | bytes 82952 | tf_op jit(solution)/shard_map/ppermute | solution.py:24
  23.5 5.9 %copy-start.7 = (f32[2,1,48,1152]{3,2,1,0:T(8,128)S(1)}, f32[2,1,48,1152]{3,2,1,0:T(8,128)}, u32[]{:S(2)}) copy-start(f32[2,1,48,1152]{3,2,1,0:T(8,128)} %param.7) | copy-start | bytes 1327108
  23.8 6.0 %collective-permute-start.3 = (f32[2,1,3,1152]{3,2,1,0:T(4,128)S(1)}, f32[2,1,3,1152]{3,2,1,0:T(4,128)S(1)}, u32[]{:S(2)}, u32[]{:S(2)}) collective-permute-start(f32[2,1,3,1152]{3,2,1,0:T(4,128)S(1)} %get-tuple-element.42), channel_id=1, source_target_pairs={{0,4},{4,8},{8,12},{12,16},{16,20},{20,24},{24,28},{1,5},{5,9},{9,... | collective-permute-start | bytes 82952 | tf_op jit(solution)/shard_map/ppermute | solution.py:21
  28.1 5.9 %collective-permute-start.4 = (f32[2,1,3,1152]{3,2,1,0:T(4,128)S(1)}, f32[2,1,3,1152]{3,2,1,0:T(4,128)S(1)}, u32[]{:S(2)}, u32[]{:S(2)}) collective-permute-start(f32[2,1,3,1152]{3,2,1,0:T(4,128)S(1)} %get-tuple-element.43), channel_id=1, source_target_pairs={{4,0},{8,4},{12,8},{16,12},{20,16},{24,20},{28,24},{5,1},{9,5},{13... | collective-permute-start | bytes 82952 | tf_op jit(solution)/shard_map/ppermute | solution.py:24
  36.7 5.5 %collective-permute-start.5 = (f32[2,1,3,1152]{3,2,1,0:T(4,128)S(1)}, f32[2,1,3,1152]{3,2,1,0:T(4,128)S(1)}, u32[]{:S(2)}, u32[]{:S(2)}) collective-permute-start(f32[2,1,3,1152]{3,2,1,0:T(4,128)S(1)} %get-tuple-element.38), channel_id=1, source_target_pairs={{0,4},{4,8},{8,12},{12,16},{16,20},{20,24},{24,28},{1,5},{5,9},{9,... | collective-permute-start | bytes 82952 | tf_op jit(solution)/shard_map/ppermute | solution.py:21
  40.1 5.9 %collective-permute-start.6 = (f32[2,1,3,1152]{3,2,1,0:T(4,128)S(1)}, f32[2,1,3,1152]{3,2,1,0:T(4,128)S(1)}, u32[]{:S(2)}, u32[]{:S(2)}) collective-permute-start(f32[2,1,3,1152]{3,2,1,0:T(4,128)S(1)} %get-tuple-element.39), channel_id=1, source_target_pairs={{4,0},{8,4},{12,8},{16,12},{20,16},{24,20},{28,24},{5,1},{9,5},{13... | collective-permute-start | bytes 82952 | tf_op jit(solution)/shard_map/ppermute | solution.py:24
  48.5 5.9 %copy-start.8 = (f32[1,2,1,48,288]{4,3,1,2,0:T(8,128)S(1)}, f32[1,2,1,48,288]{4,3,1,2,0:T(8,128)}, u32[]{:S(2)}) copy-start(f32[1,2,1,48,288]{4,3,1,2,0:T(8,128)} %slice_bitcast_fusion.3) | copy-start | bytes 331780
  48.7 10.9 %collective-permute-start.7 = (f32[2,1,3,1152]{3,2,1,0:T(4,128)S(1)}, f32[2,1,3,1152]{3,2,1,0:T(4,128)S(1)}, u32[]{:S(2)}, u32[]{:S(2)}) collective-permute-start(f32[2,1,3,1152]{3,2,1,0:T(4,128)S(1)} %get-tuple-element.34), channel_id=1, source_target_pairs={{0,4},{4,8},{8,12},{12,16},{16,20},{20,24},{24,28},{1,5},{5,9},{9,... | collective-permute-start | bytes 82952 | tf_op jit(solution)/shard_map/ppermute | solution.py:21
  53.1 6.5 %collective-permute-start.8 = (f32[2,1,3,1152]{3,2,1,0:T(4,128)S(1)}, f32[2,1,3,1152]{3,2,1,0:T(4,128)S(1)}, u32[]{:S(2)}, u32[]{:S(2)}) collective-permute-start(f32[2,1,3,1152]{3,2,1,0:T(4,128)S(1)} %get-tuple-element.35), channel_id=1, source_target_pairs={{4,0},{8,4},{12,8},{16,12},{20,16},{24,20},{28,24},{5,1},{9,5},{13... | collective-permute-start | bytes 82952 | tf_op jit(solution)/shard_map/ppermute | solution.py:24
  55.3 13.7 %all-to-all-start.1 = ((f32[4,2,1,48,288]{4,3,1,2,0:T(8,128)}), f32[4,2,1,48,288]{4,3,1,2,0:T(8,128)}, u32[]{:S(2)}, u32[]{:S(2)}) async-start(f32[4,2,1,48,288]{4,3,1,2,0:T(8,128)} %pad_maximum_fusion), calls=%async_computation.1 | async-start | bytes 1179648 | tf_op jit(solution)/shard_map/all_to_all | solution.py:131
  69.0 11.4 %all-to-all-start = ((f32[4,1,27648]{2,1,0:T(1,128)}), f32[4,1,27648]{2,1,0:T(1,128)S(1)}, u32[]{:S(2)}, u32[]{:S(2)}) async-start(f32[4,1,27648]{2,1,0:T(1,128)} %reshape.594), calls=%async_computation | async-start | bytes 884736 | tf_op jit(solution)/shard_map/all_to_all | solution.py:129
  89.9 0.8 copy-start.2
  91.2 0.8 copy-start.3
  91.9 2.6 %copy-start = (f32[2,4,13824]{2,1,0:T(4,128)}, f32[2,4,13824]{2,1,0:T(4,128)S(1)}, u32[]{:S(2)}) copy-start(f32[2,4,13824]{2,1,0:T(4,128)S(1)} %get-tuple-element.6) | copy-start | bytes 1327108
  92.4 0.8 copy-start.4
  114.2 8.9 %collective-permute-start.9 = (f32[2,1,3,1152]{3,2,1,0:T(4,128)S(1)}, f32[2,1,3,1152]{3,2,1,0:T(4,128)S(1)}, u32[]{:S(2)}, u32[]{:S(2)}) collective-permute-start(f32[2,1,3,1152]{3,2,1,0:T(4,128)S(1)} %get-tuple-element.30), channel_id=1, source_target_pairs={{0,4},{4,8},{8,12},{12,16},{16,20},{20,24},{24,28},{1,5},{5,9},{9,... | collective-permute-start | bytes 82952 | tf_op jit(solution)/shard_map/ppermute | solution.py:21
  118.8 5.9 %collective-permute-start.10 = (f32[2,1,3,1152]{3,2,1,0:T(4,128)S(1)}, f32[2,1,3,1152]{3,2,1,0:T(4,128)S(1)}, u32[]{:S(2)}, u32[]{:S(2)}) collective-permute-start(f32[2,1,3,1152]{3,2,1,0:T(4,128)S(1)} %get-tuple-element.31), channel_id=1, source_target_pairs={{4,0},{8,4},{12,8},{16,12},{20,16},{24,20},{28,24},{5,1},{9,5},{13... | collective-permute-start | bytes 82952 | tf_op jit(solution)/shard_map/ppermute | solution.py:24
